TPU v7x, 32 devices: a whole 2x2x4 slice. The times are simulated.
32 devices in a mesh: dp: 8 (over z, x), tensor: 4 (over y, core).
Axes of the slice: x: 2, y: 2, z: 4, core: 2. Of those that a mesh axis runs over, the one named last changes fastest.
Arguments:
- residual_in: float32 [8, 1024, 640], P('dp', 'tensor'), may hold values from -6 to 6
- positions: int32 [8, 1024], P('dp'), may hold values from 0 to 2047
- segments: int32 [8, 1024], P('dp'), may hold values from 0 to 7, never falling along the last dimension, each value on 1 to 512 neighbouring positions
- gain_in: float32 [640], replicated, may hold values from 0.5 to 1.5
- w_query: bfloat16 [640, 1024], P(None, 'tensor'), may hold values from -1 to 1
- w_key: bfloat16 [640, 256], replicated, may hold values from -1 to 1
- w_value: bfloat16 [640, 256], replicated, may hold values from -0.25 to 0.25
- gain_query: float32 [256], replicated, may hold values from 0.5 to 4
- gain_key: float32 [256], replicated, may hold values from 0.5 to 4
- w_out: bfloat16 [1024, 640], P('tensor'), may hold values from -0.1875 to 0.1875
- gain_attn: float32 [640], replicated, may hold values from 0.5 to 1.5
- gain_pre: float32 [640], replicated, may hold values from 0.5 to 1.5
- w_gate: bfloat16 [640, 2048], P(None, 'tensor'), may hold values from -0.25 to 0.25
- w_up: bfloat16 [640, 2048], P(None, 'tensor'), may hold values from -0.25 to 0.25
- w_down: bfloat16 [2048, 640], P('tensor'), may hold values from -0.125 to 0.125
- gain_post: float32 [640], replicated, may hold values from 0.5 to 1.5
- cotangent: float32 [8, 1024, 640], P('dp', 'tensor'), may hold values from -6 to 6
Outputs:
- layer_out: float32 [8, 1024, 640], P('dp', 'tensor')
- grad_input: float32 [8, 1024, 640], P('dp', 'tensor')
- grad_gain_in: float32 [640], replicated
- grad_w_query: float32 [640, 1024], P(None, 'tensor')
- grad_w_key: float32 [640, 256], replicated
- grad_w_value: float32 [640, 256], replicated
- grad_gain_query: float32 [256], replicated
- grad_gain_key: float32 [256], replicated
- grad_w_out: float32 [1024, 640], P('tensor')
- grad_gain_attn: float32 [640], replicated
- grad_gain_pre: float32 [640], replicated
- grad_w_gate: float32 [640, 2048], P(None, 'tensor')
- grad_w_up: float32 [640, 2048], P(None, 'tensor')
- grad_w_down: float32 [2048, 640], P('tensor')
- grad_gain_post: float32 [640], replicated
Inputs may be any that keep to these rules, and one draw needn't show every extreme that they name: `segments`: ids never fall along a packed row, each document holds 1 to 512 tokens, and every row has one document of exactly 512 tokens.
All inputs are finite; a program needn't handle non-finite values.
Results may differ from a plain program's by a relative error of at most 0.02.
The roundings to bfloat16 on the way count: a program that leaves them out, or rounds other values in their place, can miss the bound.
Values may be sent and summed in bfloat16 or wider, within the bound.
No kernel may reach another device: no remote copies, remote signals or barrier semaphores. Data moves between devices by JAX's collectives and lax.ppermute only.
A program may use at most 128 MiB of HBM per device.

v0:
```python
import math

import jax
import jax.numpy as jnp
from jax import lax
from jax.sharding import PartitionSpec as P

WINDOW = 512


EPSILON = 1e-06


def rms_forward(values, gain):
    factor = lax.rsqrt(jnp.mean(values * values, axis=-1, keepdims=True) + EPSILON)
    return (values * factor * gain, factor)


def rms_backward(values, factor, gain, upstream):
    unit_vals = values * factor
    weighted = upstream * gain
    inner = jnp.mean(weighted * unit_vals, axis=-1, keepdims=True)
    back = factor * (weighted - unit_vals * inner)
    gain_grad = jnp.sum((upstream * unit_vals).reshape(-1, values.shape[-1]), axis=0)
    return (back, gain_grad)


def rope_tables(spots, width):
    half_width = width // 2
    inverse = jnp.exp(
        jnp.arange(half_width, dtype=jnp.float32) * (-2.0 * math.log(10000.0) / width)
    )
    angles = spots.astype(jnp.float32)[:, None] * inverse[None, :]
    return (jnp.cos(angles), jnp.sin(angles))


def rotate(values, cosine, sine_part):
    half_width = values.shape[-1] // 2
    first = values[..., :half_width]
    second = values[..., half_width:]
    return jnp.concatenate(
        [first * cosine - second * sine_part, second * cosine + first * sine_part], axis=-1
    )


def gelu_parts(values):
    coeff = math.sqrt(2.0 / math.pi)
    tangent = jnp.tanh(coeff * (values + 0.044715 * values * values * values))
    output = 0.5 * values * (1.0 + tangent)
    slope = 0.5 * (1.0 + tangent) + 0.5 * values * (1.0 - tangent * tangent) * coeff * (
        1.0 + 3.0 * 0.044715 * values * values
    )
    return (output, slope)


def key_windows(values, filler):
    lead = jnp.full((WINDOW,) + values.shape[1:], filler, values.dtype)
    padded = jnp.concatenate([lead, values], axis=0)
    blocks = values.shape[0] // WINDOW
    block_shape = (blocks, WINDOW) + values.shape[1:]
    return jnp.concatenate(
        [padded[:-WINDOW].reshape(block_shape), values.reshape(block_shape)], axis=1
    )


def allowed_mask(docs_query, docs_key):
    row_index = lax.broadcasted_iota(jnp.int32, (WINDOW, 2 * WINDOW), 0)
    col_index = lax.broadcasted_iota(jnp.int32, (WINDOW, 2 * WINDOW), 1)
    same_doc = docs_query[:, None] == docs_key[None, :]
    return same_doc & (col_index > row_index) & (col_index <= row_index + WINDOW)


def block_scores(query_blk, key_blk, docs_query, docs_key):
    raw_scores = jnp.einsum(
        "qhd,kd->hqk", query_blk, key_blk, preferred_element_type=jnp.float32
    ) / math.sqrt(query_blk.shape[-1])
    return jnp.where(allowed_mask(docs_query, docs_key)[None], raw_scores, -1e30)


def attend_block(operands):
    query_blk, key_blk, value_blk, docs_query, docs_key = operands
    scores = block_scores(query_blk, key_blk, docs_query, docs_key)
    highest = jnp.max(scores, axis=-1, keepdims=True)
    log_total = highest + jnp.log(jnp.sum(jnp.exp(scores - highest), axis=-1, keepdims=True))
    probs = jnp.exp(scores - log_total).astype(jnp.bfloat16)
    attended = jnp.einsum(
        "hqk,kd->qhd", probs, value_blk, preferred_element_type=jnp.float32
    ).astype(jnp.bfloat16)
    return (attended, log_total[..., 0])


def attend_back(operands):
    query_blk, key_blk, value_blk, docs_query, docs_key, log_total, upstream = operands
    scores = block_scores(query_blk, key_blk, docs_query, docs_key)
    probs = jnp.exp(scores - log_total[..., None])
    probs_low = probs.astype(jnp.bfloat16)
    dprob = jnp.einsum("qhd,kd->hqk", upstream, value_blk, preferred_element_type=jnp.float32)
    delta = jnp.sum(probs * dprob, axis=-1, keepdims=True)
    dscore = (probs * (dprob - delta) / math.sqrt(query_blk.shape[-1])).astype(jnp.bfloat16)
    grad_query = jnp.einsum("hqk,kd->qhd", dscore, key_blk, preferred_element_type=jnp.float32)
    grad_key = jnp.einsum("hqk,qhd->khd", dscore, query_blk, preferred_element_type=jnp.float32)
    grad_value = jnp.einsum("hqk,qhd->khd", probs_low, upstream, preferred_element_type=jnp.float32)
    return (grad_query, grad_key, grad_value)


def spread_keys(parts):
    early = parts[:, :WINDOW]
    late = parts[:, WINDOW:]
    moved = jnp.concatenate([early[1:], jnp.zeros_like(early[:1])], axis=0)
    return (late + moved).reshape((-1,) + parts.shape[2:])


def attention_forward(query_rot, key_rot, value_low, docs):
    blocks = query_rot.shape[0] // WINDOW
    operands = (
        query_rot.reshape((blocks, WINDOW) + query_rot.shape[1:]),
        key_windows(key_rot, 0),
        key_windows(value_low, 0),
        docs.reshape(blocks, WINDOW),
        key_windows(docs, -1),
    )
    attended, log_total = lax.map(attend_block, operands)
    return (attended.reshape(query_rot.shape), log_total, operands)


def attention_backward(operands, log_total, upstream):
    blocks = upstream.shape[0] // WINDOW
    upstream_blocks = upstream.reshape((blocks, WINDOW) + upstream.shape[1:])
    grad_query, grad_key, grad_value = lax.map(attend_back, operands + (log_total, upstream_blocks))
    return (grad_query.reshape(upstream.shape), spread_keys(grad_key), spread_keys(grad_value))


def on_device(
    residual_in,
    positions,
    segments,
    gain_in,
    w_query,
    w_key,
    w_value,
    gain_query,
    gain_key,
    w_out,
    gain_attn,
    gain_pre,
    w_gate,
    w_up,
    w_down,
    gain_post,
    cotangent,
):
    residual_rows = residual_in[0]
    upstream = cotangent[0]
    spots = positions[0]
    docs = segments[0]
    width = w_key.shape[1]
    heads_here = w_query.shape[1] // width
    normed, factor_in = rms_forward(residual_rows, gain_in)
    normed_low = normed.astype(jnp.bfloat16)
    gathered = lax.all_gather(normed_low, "tensor", axis=0, tiled=True)
    total = gathered.shape[0]
    query = jnp.dot(gathered, w_query, preferred_element_type=jnp.float32).reshape(
        total, heads_here, width
    )
    keyed = jnp.dot(gathered, w_key, preferred_element_type=jnp.float32)
    valued = jnp.dot(gathered, w_value, preferred_element_type=jnp.float32)
    query_normed, factor_query = rms_forward(query, gain_query)
    key_normed, factor_key = rms_forward(keyed, gain_key)
    cosine, sine_part = rope_tables(spots, width)
    query_rot = rotate(query_normed, cosine[:, None], sine_part[:, None]).astype(jnp.bfloat16)
    key_rot = rotate(key_normed, cosine, sine_part).astype(jnp.bfloat16)
    value_low = valued.astype(jnp.bfloat16)
    attended, log_total, operands = attention_forward(query_rot, key_rot, value_low, docs)
    flat = attended.reshape(total, heads_here * width)
    branch = lax.psum_scatter(
        jnp.dot(flat, w_out, preferred_element_type=jnp.float32),
        "tensor",
        scatter_dimension=0,
        tiled=True,
    )
    post_attn, factor_attn = rms_forward(branch, gain_attn)
    middle = residual_rows + post_attn
    normed_two, factor_pre = rms_forward(middle, gain_pre)
    normed_two_low = normed_two.astype(jnp.bfloat16)
    gathered_two = lax.all_gather(normed_two_low, "tensor", axis=0, tiled=True)
    gate = jnp.dot(gathered_two, w_gate, preferred_element_type=jnp.float32)
    up_proj = jnp.dot(gathered_two, w_up, preferred_element_type=jnp.float32)
    activated, slope = gelu_parts(gate)
    hidden = (activated * up_proj).astype(jnp.bfloat16)
    ffn_out = lax.psum_scatter(
        jnp.dot(hidden, w_down, preferred_element_type=jnp.float32).astype(jnp.bfloat16),
        "tensor",
        scatter_dimension=0,
        tiled=True,
    ).astype(jnp.float32)
    post_ffn, factor_post = rms_forward(ffn_out, gain_post)
    result_rows = middle + post_ffn
    grad_ffn, grad_gain_post = rms_backward(ffn_out, factor_post, gain_post, upstream)
    ffn_grad_all = lax.all_gather(grad_ffn.astype(jnp.bfloat16), "tensor", axis=0, tiled=True)
    grad_w_down = jnp.dot(hidden.T, ffn_grad_all, preferred_element_type=jnp.float32)
    grad_hidden = jnp.dot(ffn_grad_all, w_down.T, preferred_element_type=jnp.float32)
    grad_up = (grad_hidden * activated).astype(jnp.bfloat16)
    grad_gate = (grad_hidden * up_proj * slope).astype(jnp.bfloat16)
    grad_w_gate = jnp.dot(gathered_two.T, grad_gate, preferred_element_type=jnp.float32)
    grad_w_up = jnp.dot(gathered_two.T, grad_up, preferred_element_type=jnp.float32)
    grad_w_gate, grad_w_up, grad_w_down = lax.psum((grad_w_gate, grad_w_up, grad_w_down), "dp")
    grad_normed_two = lax.psum_scatter(
        (
            jnp.dot(grad_gate, w_gate.T, preferred_element_type=jnp.float32)
            + jnp.dot(grad_up, w_up.T, preferred_element_type=jnp.float32)
        ).astype(jnp.bfloat16),
        "tensor",
        scatter_dimension=0,
        tiled=True,
    ).astype(jnp.float32)
    back_pre, grad_gain_pre = rms_backward(middle, factor_pre, gain_pre, grad_normed_two)
    grad_middle = upstream + back_pre
    grad_branch, grad_gain_attn = rms_backward(branch, factor_attn, gain_attn, grad_middle)
    attn_grad_all = lax.all_gather(grad_branch.astype(jnp.bfloat16), "tensor", axis=0, tiled=True)
    grad_w_out = jnp.dot(flat.T, attn_grad_all, preferred_element_type=jnp.float32)
    grad_attended = (
        jnp.dot(attn_grad_all, w_out.T, preferred_element_type=jnp.float32)
        .astype(jnp.bfloat16)
        .reshape(total, heads_here, width)
    )
    grad_query_rot, grad_key_rot, grad_value = attention_backward(
        operands, log_total, grad_attended
    )
    grad_query, grad_gain_query = rms_backward(
        query,
        factor_query,
        gain_query,
        rotate(grad_query_rot, cosine[:, None], -sine_part[:, None]),
    )
    grad_key, grad_gain_key = rms_backward(
        keyed[:, None],
        factor_key[:, None],
        gain_key,
        rotate(grad_key_rot, cosine[:, None], -sine_part[:, None]),
    )
    query_low = grad_query.reshape(total, heads_here * width).astype(jnp.bfloat16)
    key_low = grad_key.astype(jnp.bfloat16)
    value_grad_low = grad_value.astype(jnp.bfloat16)
    grad_w_query = jnp.dot(gathered.T, query_low, preferred_element_type=jnp.float32)
    grad_w_key = jnp.einsum("td,thk->dk", gathered, key_low, preferred_element_type=jnp.float32)
    grad_w_value = jnp.einsum(
        "td,thk->dk", gathered, value_grad_low, preferred_element_type=jnp.float32
    )
    grad_normed = lax.psum_scatter(
        (
            jnp.dot(query_low, w_query.T, preferred_element_type=jnp.float32)
            + jnp.einsum("thk,dk->td", key_low, w_key, preferred_element_type=jnp.float32)
            + jnp.einsum("thk,dk->td", value_grad_low, w_value, preferred_element_type=jnp.float32)
        ).astype(jnp.bfloat16),
        "tensor",
        scatter_dimension=0,
        tiled=True,
    ).astype(jnp.float32)
    back_in, grad_gain_in = rms_backward(residual_rows, factor_in, gain_in, grad_normed)
    grad_rows = grad_middle + back_in
    grad_w_query, grad_w_out = lax.psum((grad_w_query, grad_w_out), "dp")
    (
        grad_w_key,
        grad_w_value,
        grad_gain_query,
        grad_gain_key,
        grad_gain_in,
        grad_gain_attn,
        grad_gain_pre,
        grad_gain_post,
    ) = lax.psum(
        (
            grad_w_key,
            grad_w_value,
            grad_gain_query,
            grad_gain_key,
            grad_gain_in,
            grad_gain_attn,
            grad_gain_pre,
            grad_gain_post,
        ),
        ("dp", "tensor"),
    )
    return (
        result_rows[None],
        grad_rows[None],
        grad_gain_in,
        grad_w_query,
        grad_w_key,
        grad_w_value,
        grad_gain_query,
        grad_gain_key,
        grad_w_out,
        grad_gain_attn,
        grad_gain_pre,
        grad_w_gate,
        grad_w_up,
        grad_w_down,
        grad_gain_post,
    )


def solution(mesh):
    placed = (
        P("dp", "tensor", None),
        P("dp", None),
        P("dp", None),
        P(),
        P(None, "tensor"),
        P(),
        P(),
        P(),
        P(),
        P("tensor", None),
        P(),
        P(),
        P(None, "tensor"),
        P(None, "tensor"),
        P("tensor", None),
        P(),
        P("dp", "tensor", None),
    )
    return jax.shard_map(
        on_device,
        mesh=mesh,
        in_specs=placed,
        out_specs=(
            P("dp", "tensor", None),
            P("dp", "tensor", None),
            P(),
            P(None, "tensor"),
            P(),
            P(),
            P(),
            P(),
            P("tensor", None),
            P(),
            P(),
            P(None, "tensor"),
            P(None, "tensor"),
            P("tensor", None),
            P(),
        ),
        check_vma=False,
    )
```

profile of v0, /device:TPU:0, one launch (start us, length us, event | category | flops | bytes accessed | tf_op | source)
XLA Modules:
  0.0 635.0 jit_solution(3140083096600548051)
XLA Ops:
  8.5 2.0 multiply_convert_fusion.6
  13.9 17.7 %all-gather.5.cloned.1.call-done = bf16[1024,640]{1,0:T(8,128)(2,1)} async-done(((bf16[256,640]{1,0:T(8,128)(2,1)}), bf16[1024,640]{1,0:T(8,128)(2,1)}) %all-gather.5.cloned.1.call-update) | async-done | bytes 1310736 | tf_op jit(solution)/shard_map/all_gather | solution.py:160
  31.6 2.0 convolution_convert_fusion.3
  35.5 2.4 fusion.111
  38.1 2.4 fusion.99
  41.4 1.5 pad_maximum_fusion
  42.9 8.2 %while.26 = (s32[]{:T(128)}, bf16[2,512,1,256]{3,1,0,2:T(8,128)(2,1)S(1)}, f32[2,1,512]{2,1,0:T(1,128)S(1)}, bf16[2,1024,256]{2,1,0:T(8,128)(2,1)}, s32[2,512]{1...) while((s32[]{:T(128)}, ...), condition=%wide.region_6.7_spmd, body=%wide.region_3.6_spmd.sunk | while | flops 543293440 | bytes 8955001 | solution.py:122
  42.9 1.9 fusion.191
  45.2 1.5 fusion.192
  47.0 1.9 fusion.191
  49.3 1.5 fusion.192
  51.8 2.1 fusion.117
  54.0 34.6 %reduce-scatter.5.cloned.1.call-done = f32[256,640]{1,0:T(8,128)} async-done(((f32[1024,640]{1,0:T(8,128)}), f32[256,640]{1,0:T(8,128)}) %reduce-scatter.5.cloned.1.call-update) | async-done | bytes 655376 | tf_op jit(solution)/shard_map/reduce_scatter | solution.py:175
  92.1 18.3 %all-gather.7.cloned.1.call-done = bf16[1024,640]{1,0:T(8,128)(2,1)} async-done(((bf16[256,640]{1,0:T(8,128)(2,1)}), bf16[1024,640]{1,0:T(8,128)(2,1)}) %all-gather.7.cloned.1.call-update) | async-done | bytes 1310736 | tf_op jit(solution)/shard_map/all_gather | solution.py:185
  110.4 2.4 fusion.118
  112.8 2.6 multiply_convert_fusion.1
  115.5 2.0 convolution_convert_fusion.1
  117.6 26.5 %reduce-scatter.7.cloned.1.call-done = bf16[256,640]{1,0:T(8,128)(2,1)} async-done(((bf16[1024,640]{1,0:T(8,128)(2,1)}), bf16[256,640]{1,0:T(8,128)(2,1)}) %reduce-scatter.7.cloned.1.call-update) | async-done | bytes 327696 | tf_op jit(solution)/shard_map/reduce_scatter | solution.py:190
  146.6 1.9 fusion.92
  148.7 18.1 %all-gather.9.cloned.1.call-done = bf16[1024,640]{1,0:T(8,128)(2,1)} async-done(((bf16[256,640]{1,0:T(8,128)(2,1)}), bf16[1024,640]{1,0:T(8,128)(2,1)}) %all-gather.9.cloned.1.call-update) | async-done | bytes 1310736 | tf_op jit(solution)/shard_map/all_gather | solution.py:199
  166.8 4.2 multiply_convert_fusion
  172.7 2.1 add_convert_fusion.1
  174.8 26.5 %reduce-scatter.9.cloned.1.call-done = bf16[256,640]{1,0:T(8,128)(2,1)} async-done(((bf16[1024,640]{1,0:T(8,128)(2,1)}), bf16[256,640]{1,0:T(8,128)(2,1)}) %reduce-scatter.9.cloned.1.call-update) | async-done | bytes 327696 | tf_op jit(solution)/shard_map/reduce_scatter | solution.py:207
  202.7 2.4 multiply_reduce_fusion.6
  206.9 18.2 %all-gather.11.cloned.1.call-done = bf16[1024,640]{1,0:T(8,128)(2,1)} async-done(((bf16[256,640]{1,0:T(8,128)(2,1)}), bf16[1024,640]{1,0:T(8,128)(2,1)}) %all-gather.11.cloned.1.call-update) | async-done | bytes 1310736 | tf_op jit(solution)/shard_map/all_gather | solution.py:219
  225.1 2.7 convolution_convert_fusion.2
  227.9 25.1 %while.27 = (s32[]{:T(128)}, f32[2,512,1,256]{3,1,0,2:T(8,128)}, f32[2,1024,1,256]{1,3,2,0:T(8,128)}, f32[2,1024,1,256]{3,1,0,2:T(8,128)}, bf16[2,1024,256]{2,1,...) while((s32[]{:T(128)}, f32[2,512,1,256]{3,1,0,2:T(8,128)}, ...), condition=%wide.region_18.19_spmd, body=%wide.region_16.18_spmd.sunk | while | flops 1350041600 | bytes 44076240 | solution.py:129
  227.9 1.6 fusion.201
  229.5 2.2 fusion.202
  232.2 1.5 convolution_bitcast_fusion.6
  234.0 1.5 convolution_bitcast_fusion.5
  236.6 2.4 fusion.204
  240.4 1.6 fusion.201
  242.0 2.2 fusion.202
  246.6 1.5 convolution_bitcast_fusion.5
  249.1 2.4 fusion.204
  256.1 3.9 fusion.107
  264.0 1.7 add_convert_fusion
  266.0 3.5 fusion.128
  269.5 1.9 fusion.127
  274.2 3.7 fusion.126
  280.8 11.5 %reduce-scatter.11.cloned.1.call-done = bf16[256,640]{1,0:T(8,128)(2,1)} async-done(((bf16[1024,640]{1,0:T(8,128)(2,1)}), bf16[256,640]{1,0:T(8,128)(2,1)}) %reduce-scatter.11.cloned.1.call-update) | async-done | bytes 327696 | tf_op jit(solution)/shard_map/reduce_scatter | solution.py:249
  293.5 40.3 %all-reduce.5 = (f32[640]{0:T(1024)}, f32[256]{0:T(256)}, f32[256]{0:T(256)}, f32[640]{0:T(1024)}, f32[640]{0:T(1024)}, /*index=5*/f32[640]{0:T(1024)}) all-reduce(f32[640]{0:T(1024)S(1)} %get-tuple-element.154, f32[256]{0:T(256)S(1)} %get-tuple-element.146, ...), channel_id=1, replica_groups=mesh['dp'=8,'tensor'=4] {'dp','tensor'}, use_global_device_ids=true, to_apply=%region_24.25 | all-reduce | flops 3072 | bytes 24576 | tf_op jit(solution)/shard_map/psum | solution.py:271
  333.8 2.0 fusion.83
  335.8 95.1 %all-reduce.11.cloned.1.call-done = (f32[640,256]{1,0:T(8,128)}, f32[640,256]{1,0:T(8,128)}) async-done(((f32[640,256]{1,0:T(8,128)}, f32[640,256]{1,0:T(8,128)}), (f32[640,256]{1,0:T(8,128)}, f32[640,256]{1,0:T(8,128)})) %all-reduce.11.cloned.1.call-update) | async-done | bytes 1310736 | tf_op jit(solution)/shard_map/psum | solution.py:271
  430.9 188.2 %all-reduce.13.cloned.1.call-done = (f32[640,256]{1,0:T(8,128)}, f32[256,640]{1,0:T(8,128)}, f32[640,512]{1,0:T(8,128)}, f32[640,512]{1,0:T(8,128)}, f32[512,640]{1,0:T(8,128)}) async-done(((f32[640,256]{1,0:T(8,128)}, f32[256,640]{1,0:T(8,128)}, f32[640,512]{1,0:T(8,128)}, f32[640,512]{1,0:T(8,128)}, f32[512,640]{1,0:T(8,128)}), (f32[640,256]{1,0:T(8,128)}, f32[256,640]{1,0:T(8,128)}, ...) | async-done | bytes 5242896 | tf_op jit(solution)/shard_map/psum | solution.py:261
  619.2 2.0 copy.115
  621.2 2.1 copy.116
  (222 shorter events, 47.7 us)
Async XLA Ops:
  7.2 108.3 %copy-start = (bf16[512,640]{1,0:T(8,128)(2,1)S(1)}, bf16[512,640]{1,0:T(8,128)(2,1)}, u32[]{:S(2)}) copy-start(bf16[512,640]{1,0:T(8,128)(2,1)} %param.35) | copy-start | bytes 1966084
  7.2 24.4 %all-gather.5.cloned.1.call-start = ((), (), s32[]{:S(2)}) async-start(), calls=%async_computation.4 | async-start | bytes 1638400 | tf_op jit(solution)/shard_map/all_gather | solution.py:160
  8.5 25.2 %copy-start.22 = (bf16[640,256]{1,0:T(8,128)(2,1)S(1)}, bf16[640,256]{1,0:T(8,128)(2,1)}, u32[]{:S(2)}) copy-start(bf16[640,256]{1,0:T(8,128)(2,1)} %param.25) | copy-start | bytes 983044
  10.5 78.0 %reduce-scatter.5.cloned.1.call-start = ((), (), s32[]{:S(2)}) async-start(), calls=%async_computation.5 | async-start | bytes 3276800 | tf_op jit(solution)/shard_map/reduce_scatter | solution.py:175
  31.6 2.1 copy-start.13
  35.3 2.9 copy-start.4
  35.3 2.6 copy-start.43
  42.9 9.0 %copy-start.37 = (bf16[256,640]{1,0:T(8,128)(2,1)S(1)}, bf16[256,640]{1,0:T(8,128)(2,1)}, u32[]{:S(2)}) copy-start(bf16[256,640]{1,0:T(8,128)(2,1)} %param.30) | copy-start | bytes 983044
  53.9 35.9 %copy-start.6 = (f32[1,256,640]{2,1,0:T(8,128)S(1)}, f32[1,256,640]{2,1,0:T(8,128)}, u32[]{:S(2)}) copy-start(f32[1,256,640]{2,1,0:T(8,128)} %param.21) | copy-start | bytes 1966084
  53.9 35.9 %copy-start.41 = (f32[640]{0:T(1024)S(1)}, f32[640]{0:T(1024)}, u32[]{:S(2)}) copy-start(f32[640]{0:T(1024)} %param.31) | copy-start | bytes 7684
  53.9 37.3 %copy-start.39 = (f32[640]{0:T(1024)S(1)}, f32[640]{0:T(1024)}, u32[]{:S(2)}) copy-start(f32[640]{0:T(1024)} %param.32) | copy-start | bytes 7684
  53.9 56.5 %copy-start.32 = (bf16[640,512]{1,0:T(8,128)(2,1)S(1)}, bf16[640,512]{1,0:T(8,128)(2,1)}, u32[]{:S(2)}) copy-start(bf16[640,512]{1,0:T(8,128)(2,1)} %param.33) | copy-start | bytes 1966084
  53.9 56.5 %all-gather.7.cloned.1.call-start = ((), (), s32[]{:S(2)}) async-start(), calls=%async_computation.6 | async-start | bytes 1638400 | tf_op jit(solution)/shard_map/all_gather | solution.py:185
  92.1 20.7 %copy-start.34 = (bf16[640,512]{1,0:T(8,128)(2,1)S(1)}, bf16[640,512]{1,0:T(8,128)(2,1)}, u32[]{:S(2)}) copy-start(bf16[640,512]{1,0:T(8,128)(2,1)} %param.34) | copy-start | bytes 1966084
  92.1 52.0 %reduce-scatter.7.cloned.1.call-start = ((), (), s32[]{:S(2)}) async-start(), calls=%async_computation.7 | async-start | bytes 1638400 | tf_op jit(solution)/shard_map/reduce_scatter | solution.py:190
  110.4 2.4 copy-start.45
  112.8 2.6 copy-start.48
  115.5 2.1 copy-start.49
  115.5 29.8 %copy-start.9 = (f32[1,256,640]{2,1,0:T(8,128)S(1)}, f32[1,256,640]{2,1,0:T(8,128)}, u32[]{:S(2)}) copy-start(f32[1,256,640]{2,1,0:T(8,128)} %param.37) | copy-start | bytes 1966084
  115.5 29.8 %copy-start.40 = (f32[640]{0:T(1024)S(1)}, f32[640]{0:T(1024)}, u32[]{:S(2)}) copy-start(f32[640]{0:T(1024)} %param.36) | copy-start | bytes 7684
  117.6 49.2 %all-gather.9.cloned.1.call-start = ((), (), s32[]{:S(2)}) async-start(), calls=%async_computation.8 | async-start | bytes 1638400 | tf_op jit(solution)/shard_map/all_gather | solution.py:199
  148.5 52.9 %reduce-scatter.9.cloned.1.call-start = ((), (), s32[]{:S(2)}) async-start(), calls=%async_computation.9 | async-start | bytes 1638400 | tf_op jit(solution)/shard_map/reduce_scatter | solution.py:207
  166.8 4.3 copy-start.33
  174.7 27.9 %copy-start.8 = (f32[256,640]{1,0:T(8,128)S(1)}, f32[256,640]{1,0:T(8,128)}, u32[]{:S(2)}) copy-start(f32[256,640]{1,0:T(8,128)} %reduce-scatter.5.cloned.1.call-done) | copy-start | bytes 1966084
  174.7 27.9 %copy-start.12 = (bf16[256,640]{1,0:T(8,128)(2,1)S(1)}, bf16[256,640]{1,0:T(8,128)(2,1)}, u32[]{:S(2)}) copy-start(bf16[256,640]{1,0:T(8,128)(2,1)} %reduce-scatter.7.cloned.1.call-done) | copy-start | bytes 983044
  174.8 50.4 %all-gather.11.cloned.1.call-start = ((), (), s32[]{:S(2)}) async-start(), calls=%async_computation.10 | async-start | bytes 1638400 | tf_op jit(solution)/shard_map/all_gather | solution.py:219
  202.7 22.5 %copy-start.38 = (bf16[256,640]{1,0:T(8,128)(2,1)S(1)}, bf16[256,640]{1,0:T(8,128)(2,1)}, u32[]{:S(2)}) copy-start(bf16[256,640]{1,0:T(8,128)(2,1)} %param.30) | copy-start | bytes 983044
  206.8 85.4 %reduce-scatter.11.cloned.1.call-start = ((), (), s32[]{:S(2)}) async-start(), calls=%async_computation.11 | async-start | bytes 1638400 | tf_op jit(solution)/shard_map/reduce_scatter | solution.py:249
  235.7 3.3 copy-start.24
  248.3 3.3 copy-start.24
  253.0 2.5 copy-start.26
  256.1 3.9 copy-start.5
  263.9 2.0 copy-start.47
  265.7 165.3 %all-reduce.11.cloned.1.call-start = ((), (), s32[]{:S(2)}) async-start(), calls=%async_computation.12 | async-start | bytes 2621440 | tf_op jit(solution)/shard_map/psum | solution.py:271
  265.9 3.5 copy-start.29
  266.0 3.5 copy-start.46
  269.5 1.9 copy-start.14
  274.2 3.8 copy-start.16
  274.2 345.0 %all-reduce.13.cloned.1.call-start = ((), (), s32[]{:S(2)}) async-start(), calls=%async_computation.13 | async-start | bytes 10485760 | tf_op jit(solution)/shard_map/psum | solution.py:261
  274.2 3.7 copy-start.17
  280.8 11.5 %copy-start.7 = (f32[1,256,640]{2,1,0:T(8,128)S(1)}, f32[1,256,640]{2,1,0:T(8,128)}, u32[]{:S(2)}) copy-start(f32[1,256,640]{2,1,0:T(8,128)} %param.21) | copy-start | bytes 1966084
  280.8 11.5 %copy-start.42 = (f32[640]{0:T(1024)S(1)}, f32[640]{0:T(1024)}, u32[]{:S(2)}) copy-start(f32[640]{0:T(1024)} %param.24) | copy-start | bytes 7684
  280.8 53.0 %copy-start.11 = (f32[256,640]{1,0:T(8,128)S(1)}, f32[256,640]{1,0:T(8,128)}, u32[]{:S(2)}) copy-start(f32[256,640]{1,0:T(8,128)} %copy-done.10) | copy-start | bytes 1966084
  430.9 192.3 %copy-start.30 = (f32[640,256]{1,0:T(8,128)S(1)}, f32[640,256]{1,0:T(8,128)}, u32[]{:S(2)}) copy-start(f32[640,256]{1,0:T(8,128)} %get-tuple-element.427) | copy-start | bytes 1966084
  619.2 4.9 copy-start.31
  621.2 3.8 copy-start.20
  625.0 2.1 copy-start.18
  625.0 3.2 copy-start.1
  (14 other events, 17.0 us)
Sparse Core Ops, SparseCore 0:
  10.7 20.8 all-gather.4
  54.1 34.4 reduce-scatter.4
  92.2 18.1 all-gather.6
  117.7 26.4 reduce-scatter.6
  148.6 18.1 all-gather.8
  174.9 26.4 reduce-scatter.8
  206.9 18.1 all-gather.10
  265.8 26.4 reduce-scatter.10
  298.4 132.5 all-reduce.10
  436.3 182.8 all-reduce.12
where the time goes:
time: 636 us; the launch traced here: 635 us
  waiting for transfers between devices  455 us (72%)
  matrix products  65.3 us (10%)
  blocking collectives  40.3 us (6%)
  other arithmetic  37.2 us (6%)
  local copies, waits for them, and re-layouts  21.4 us (3%)
  between operations  14.8 us (2%)
    psum x1, waiting for transfers between devices, on_device(): grad_w_query, grad_w_out = lax.psum((grad_w_query, grad_w_out), 'dp')  188 us
    psum x1, waiting for transfers between devices, on_device(): lax.psum((grad_w_key, grad_w_value, grad_gain_query, grad_gain_key, grad_...  95.1 us
    psum x1, blocking collectives, on_device(): lax.psum((grad_w_key, grad_w_value, grad_gain_query, grad_gain_key, grad_...  40.3 us
    reduce_scatter x1, waiting for transfers between devices, on_device(): lax.psum_scatter(jnp.dot(flat, w_out, preferred_element_type=jnp.float32)...  34.6 us
    reduce_scatter x1, waiting for transfers between devices, on_device(): lax.psum_scatter((jnp.dot(grad_gate, w_gate.T, preferred_element_type=jnp...  26.5 us
    reduce_scatter x1, waiting for transfers between devices, on_device(): lax.psum_scatter(jnp.dot(hidden, w_down, preferred_element_type=jnp.float...  26.5 us
    all_gather x1, waiting for transfers between devices, on_device(): gathered_two = lax.all_gather(normed_two_low, 'tensor', axis=0, tiled=True)  18.3 us
    all_gather x1, waiting for transfers between devices, on_device(): lax.all_gather(grad_branch.astype(jnp.bfloat16), 'tensor', axis=0, tiled=...  18.2 us
  transfers between devices with their start and end apart: 10, of which 10 were waited for; matrix products, arithmetic and copies ran while one was open for 3% of the time, Pallas kernels for 0%

commit v1 on v0

v1 whole, which is shorter than its diff:
```python
import math

import jax
import jax.numpy as jnp
from jax import lax
from jax.sharding import PartitionSpec as P

WINDOW = 512

EPSILON = 1e-06

LOW = jnp.bfloat16
WIDE = jnp.float32


def rms_forward(values, gain):
    factor = lax.rsqrt(jnp.mean(values * values, axis=-1, keepdims=True) + EPSILON)
    return (values * factor * gain, factor)


def rms_backward(values, factor, gain, upstream):
    unit_vals = values * factor
    weighted = upstream * gain
    inner = jnp.mean(weighted * unit_vals, axis=-1, keepdims=True)
    back = factor * (weighted - unit_vals * inner)
    gain_grad = jnp.sum((upstream * unit_vals).reshape(-1, values.shape[-1]), axis=0)
    return (back, gain_grad)


def rope_tables(spots, width):
    half_width = width // 2
    inverse = jnp.exp(
        jnp.arange(half_width, dtype=jnp.float32) * (-2.0 * math.log(10000.0) / width)
    )
    angles = spots.astype(jnp.float32)[:, None] * inverse[None, :]
    return (jnp.cos(angles), jnp.sin(angles))


def rotate(values, cosine, sine_part):
    half_width = values.shape[-1] // 2
    first = values[..., :half_width]
    second = values[..., half_width:]
    return jnp.concatenate(
        [first * cosine - second * sine_part, second * cosine + first * sine_part], axis=-1
    )


def gelu_parts(values):
    coeff = math.sqrt(2.0 / math.pi)
    tangent = jnp.tanh(coeff * (values + 0.044715 * values * values * values))
    output = 0.5 * values * (1.0 + tangent)
    slope = 0.5 * (1.0 + tangent) + 0.5 * values * (1.0 - tangent * tangent) * coeff * (
        1.0 + 3.0 * 0.044715 * values * values
    )
    return (output, slope)


def mm(left, right):
    return jnp.dot(left, right, preferred_element_type=WIDE)


def mm_nt(left, right):
    return lax.dot_general(left, right, (((1,), (1,)), ((), ())), preferred_element_type=WIDE)


def mm_tn(left, right):
    return lax.dot_general(left, right, (((0,), (0,)), ((), ())), preferred_element_type=WIDE)


def swap(values, axis, size, bit):
    return lax.ppermute(values, axis, [(i, i ^ bit) for i in range(size)])


def add_low(mine, other):
    return (mine.astype(WIDE) + other.astype(WIDE)).astype(LOW)


def bits_of(size):
    if size & (size - 1):
        raise ValueError("axis size")
    return [1 << i for i in range(size.bit_length() - 1)]


def halves(values, upper):
    rows = values.shape[0] // 2
    keep = lax.dynamic_slice_in_dim(values, upper * rows, rows, 0)
    send = lax.dynamic_slice_in_dim(values, (1 - upper) * rows, rows, 0)
    return keep, send


def scatter_sum(values, axis, size):
    place = lax.axis_index(axis)
    for bit in bits_of(size):
        upper = (place & bit) // bit
        keep, send = halves(values, upper)
        values = add_low(keep, swap(send, axis, size, bit))
    return values


def gather_back(values, axis, size):
    place = lax.axis_index(axis)
    for bit in reversed(bits_of(size)):
        upper = (place & bit) // bit
        other = swap(values, axis, size, bit)
        low_first = jnp.concatenate([values, other], axis=0)
        high_first = jnp.concatenate([other, values], axis=0)
        values = jnp.where(upper == 0, low_first, high_first)
    return values


def all_sum(values, axis, size):
    for bit in bits_of(size):
        values = values + swap(values, axis, size, bit)
    return values


def build(n_dp, n_tensor):
    near, far = 1, n_tensor // 2
    if n_tensor != 4:
        raise ValueError("tensor size")

    def beside(values):
        return swap(values, "tensor", n_tensor, near)

    def across(values):
        return swap(values, "tensor", n_tensor, far)

    def pair_sum(partial, wire):
        rows = partial.shape[0] // 2
        return partial[:rows] + beside(partial[rows:].astype(wire)).astype(WIDE)

    def pair_gather(mine):
        return jnp.concatenate([mine, beside(mine)], axis=0)

    def reduce_dp(values):
        return gather_back(scatter_sum(values, "dp", n_dp), "dp", n_dp)

    def on_device(
        residual_in,
        positions,
        segments,
        gain_in,
        w_query,
        w_key,
        w_value,
        gain_query,
        gain_key,
        w_out,
        gain_attn,
        gain_pre,
        w_gate,
        w_up,
        w_down,
        gain_post,
        cotangent,
    ):
        residual_rows = residual_in[0]
        upstream = cotangent[0]
        rows = residual_rows.shape[0]
        width = w_key.shape[1]
        me = lax.axis_index("tensor")
        order = [me, me ^ near, me ^ far, me ^ far ^ near]

        def block_of(table, which):
            return lax.dynamic_slice_in_dim(table, which * rows, rows, 0)

        w_query_far = across(w_query)
        w_out_far = across(w_out)
        w_gate_far = across(w_gate)
        w_up_far = across(w_up)
        w_down_far = across(w_down)

        spots = [block_of(positions[0], b) for b in order[:2]]
        docs = jnp.concatenate([block_of(segments[0], b) for b in order])
        token = jnp.concatenate([b * rows + jnp.arange(rows, dtype=jnp.int32) for b in order])
        cosine, sine_part = rope_tables(jnp.concatenate(spots), width)
        cos_own, sin_own = cosine[:rows], sine_part[:rows]

        normed, factor_in = rms_forward(residual_rows, gain_in)
        normed_low = normed.astype(LOW)
        keyed = mm(normed_low, w_key)
        valued = mm(normed_low, w_value)
        key_normed, factor_key = rms_forward(keyed, gain_key)
        key_rot = rotate(key_normed, cos_own, sin_own).astype(LOW)
        kv_own = jnp.concatenate([key_rot, valued.astype(LOW)], axis=1)
        kv_far = across(kv_own)
        kv_all = jnp.concatenate([kv_own, beside(kv_own), kv_far, beside(kv_far)], axis=0)
        key_all, value_all = kv_all[:, :width], kv_all[:, width:]

        chip_rows = pair_gather(normed_low)
        gap = token[: 2 * rows, None] - token[None, :]
        allowed = (docs[: 2 * rows, None] == docs[None, :]) & (gap >= 0) & (gap < WINDOW)

        scale = 1.0 / math.sqrt(width)
        saved = []
        partial = 0.0
        for w_q, w_o in ((w_query, w_out), (w_query_far, w_out_far)):
            query = mm(chip_rows, w_q)
            query_normed, factor_query = rms_forward(query, gain_query)
            query_rot = rotate(query_normed, cosine, sine_part).astype(LOW)
            scores = jnp.where(allowed, mm_nt(query_rot, key_all) * scale, -1e30)
            highest = jnp.max(scores, axis=-1, keepdims=True)
            log_total = highest + jnp.log(jnp.sum(jnp.exp(scores - highest), axis=-1, keepdims=True))
            probs = jnp.exp(scores - log_total).astype(LOW)
            attended = mm(probs, value_all).astype(LOW)
            saved.append((query, factor_query, query_rot, log_total, attended))
            partial = partial + mm(attended, w_o)
        branch = pair_sum(partial, WIDE)
        post_attn, factor_attn = rms_forward(branch, gain_attn)
        middle = residual_rows + post_attn
        normed_two, factor_pre = rms_forward(middle, gain_pre)
        chip_two = pair_gather(normed_two.astype(LOW))

        units = []
        partial = 0.0
        for w_g, w_u, w_d in ((w_gate, w_up, w_down), (w_gate_far, w_up_far, w_down_far)):
            gate = mm(chip_two, w_g)
            up_proj = mm(chip_two, w_u)
            activated, slope = gelu_parts(gate)
            hidden = (activated * up_proj).astype(LOW)
            units.append((activated, slope, up_proj, hidden))
            partial = partial + mm(hidden, w_d)
        ffn_out = pair_sum(partial, WIDE)
        post_ffn, factor_post = rms_forward(ffn_out, gain_post)
        result_rows = middle + post_ffn

        grad_ffn, grad_gain_post = rms_backward(ffn_out, factor_post, gain_post, upstream)
        chip_gf = pair_gather(grad_ffn.astype(LOW))
        back = []
        partial = 0.0
        for (w_g, w_u, w_d), (activated, slope, up_proj, hidden) in zip(
            ((w_gate_far, w_up_far, w_down_far), (w_gate, w_up, w_down)), units[::-1]
        ):
            grad_hidden = mm_nt(chip_gf, w_d)
            grad_up = (grad_hidden * activated).astype(LOW)
            grad_gate = (grad_hidden * up_proj * slope).astype(LOW)
            back.append((grad_up, grad_gate, hidden))
            partial = partial + mm_nt(grad_gate, w_g) + mm_nt(grad_up, w_u)
        (up_far, gate_far, hidden_far), (up_own, gate_own, hidden_own) = back
        down_in = across(mm_tn(hidden_far, chip_gf).astype(LOW))
        gate_in = across(mm_tn(chip_two, gate_far).astype(LOW))
        up_in = across(mm_tn(chip_two, up_far).astype(LOW))
        grad_w_down = (mm_tn(hidden_own, chip_gf) + down_in.astype(WIDE)).astype(LOW)
        grad_w_gate = (mm_tn(chip_two, gate_own) + gate_in.astype(WIDE)).astype(LOW)
        grad_w_up = (mm_tn(chip_two, up_own) + up_in.astype(WIDE)).astype(LOW)
        grad_w_down = reduce_dp(grad_w_down).astype(WIDE)
        grad_w_gate = reduce_dp(grad_w_gate).astype(WIDE)
        grad_w_up = reduce_dp(grad_w_up).astype(WIDE)

        grad_normed_two = pair_sum(partial, LOW)
        back_pre, grad_gain_pre = rms_backward(middle, factor_pre, gain_pre, grad_normed_two)
        grad_middle = upstream + back_pre
        grad_branch, grad_gain_attn = rms_backward(branch, factor_attn, gain_attn, grad_middle)
        chip_gb = pair_gather(grad_branch.astype(LOW))

        partial = 0.0
        grad_keys = 0.0
        grad_values = 0.0
        grad_gain_query = 0.0
        query_grads = []
        for (w_q, w_o), (query, factor_query, query_rot, log_total, attended) in zip(
            ((w_query_far, w_out_far), (w_query, w_out)), saved[::-1]
        ):
            grad_attended = mm_nt(chip_gb, w_o).astype(LOW)
            scores = jnp.where(allowed, mm_nt(query_rot, key_all) * scale, -1e30)
            probs = jnp.exp(scores - log_total)
            dprob = mm_nt(grad_attended, value_all)
            delta = jnp.sum(probs * dprob, axis=-1, keepdims=True)
            dscore = (probs * (dprob - delta) * scale).astype(LOW)
            grad_query_rot = mm(dscore, key_all)
            grad_keys = grad_keys + mm_tn(dscore, query_rot)
            grad_values = grad_values + mm_tn(probs.astype(LOW), grad_attended)
            grad_query, gain_part = rms_backward(
                query, factor_query, gain_query, rotate(grad_query_rot, cosine, -sine_part)
            )
            grad_gain_query = grad_gain_query + gain_part
            query_low = grad_query.astype(LOW)
            query_grads.append(query_low)
            partial = partial + mm_nt(query_low, w_q)
        out_in = across(mm_tn(saved[1][4], chip_gb).astype(LOW))
        grad_w_out = (mm_tn(saved[0][4], chip_gb) + out_in.astype(WIDE)).astype(LOW)
        grad_w_out = reduce_dp(grad_w_out).astype(WIDE)

        grad_kv = jnp.concatenate([grad_keys, grad_values], axis=1)
        mine = jnp.concatenate([grad_kv[:rows], grad_kv[2 * rows : 3 * rows]], axis=0)
        theirs = jnp.concatenate([grad_kv[rows : 2 * rows], grad_kv[3 * rows :]], axis=0)
        chip_kv = mine + beside(theirs.astype(LOW)).astype(WIDE)
        kv_total = chip_kv[:rows] + across(chip_kv[rows:].astype(LOW)).astype(WIDE)

        query_in = across(mm_tn(chip_rows, query_grads[0]).astype(LOW))
        grad_w_query = (mm_tn(chip_rows, query_grads[1]) + query_in.astype(WIDE)).astype(LOW)

        grad_key, grad_gain_key = rms_backward(
            keyed, factor_key, gain_key, rotate(kv_total[:, :width], cos_own, -sin_own)
        )
        key_low = grad_key.astype(LOW)
        value_low = kv_total[:, width:].astype(LOW)
        grad_normed = pair_sum(partial, LOW) + mm_nt(key_low, w_key) + mm_nt(value_low, w_value)
        back_in, grad_gain_in = rms_backward(residual_rows, factor_in, gain_in, grad_normed)
        grad_rows = grad_middle + back_in

        low_bit, high_bit = me & near, (me & far) // far
        both = jnp.stack([mm_tn(normed_low, key_low), mm_tn(normed_low, value_low)])
        kept = lax.dynamic_index_in_dim(both, low_bit, 0, False)
        sent = lax.dynamic_index_in_dim(both, 1 - low_bit, 0, False)
        one = kept + beside(sent.astype(LOW)).astype(WIDE)
        half = width // 2
        kept = lax.dynamic_slice_in_dim(one, high_bit * half, half, 1)
        sent = lax.dynamic_slice_in_dim(one, (1 - high_bit) * half, half, 1)
        quarter = (kept + across(sent.astype(LOW)).astype(WIDE)).astype(LOW)
        last = reduce_dp(jnp.concatenate([grad_w_query, quarter], axis=1))
        grad_w_query = last[:, : w_query.shape[1]].astype(WIDE)
        quarter = last[:, w_query.shape[1] :]
        other = across(quarter)
        one = jnp.where(
            high_bit == 0,
            jnp.concatenate([quarter, other], axis=1),
            jnp.concatenate([other, quarter], axis=1),
        )
        other = beside(one)
        grad_w_key = jnp.where(low_bit == 0, one, other).astype(WIDE)
        grad_w_value = jnp.where(low_bit == 0, other, one).astype(WIDE)

        gains = [
            grad_gain_in,
            grad_gain_attn,
            grad_gain_pre,
            grad_gain_post,
            grad_gain_query,
            grad_gain_key,
        ]
        packed = jnp.concatenate(gains).reshape(-1, 128)
        packed = all_sum(packed, "tensor", n_tensor)
        packed = all_sum(packed, "dp", n_dp).reshape(-1)
        summed = []
        start = 0
        for gain in gains:
            summed.append(packed[start : start + gain.shape[0]])
            start += gain.shape[0]
        grad_gain_in, grad_gain_attn, grad_gain_pre, grad_gain_post = summed[:4]
        grad_gain_query, grad_gain_key = summed[4:]
        return (
            result_rows[None],
            grad_rows[None],
            grad_gain_in,
            grad_w_query,
            grad_w_key,
            grad_w_value,
            grad_gain_query,
            grad_gain_key,
            grad_w_out,
            grad_gain_attn,
            grad_gain_pre,
            grad_w_gate,
            grad_w_up,
            grad_w_down,
            grad_gain_post,
        )

    return on_device


def solution(mesh):
    placed = (
        P("dp", "tensor", None),
        P("dp", None),
        P("dp", None),
        P(),
        P(None, "tensor"),
        P(),
        P(),
        P(),
        P(),
        P("tensor", None),
        P(),
        P(),
        P(None, "tensor"),
        P(None, "tensor"),
        P("tensor", None),
        P(),
        P("dp", "tensor", None),
    )
    return jax.shard_map(
        build(mesh.shape["dp"], mesh.shape["tensor"]),
        mesh=mesh,
        in_specs=placed,
        out_specs=(
            P("dp", "tensor", None),
            P("dp", "tensor", None),
            P(),
            P(None, "tensor"),
            P(),
            P(),
            P(),
            P(),
            P("tensor", None),
            P(),
            P(),
            P(None, "tensor"),
            P(None, "tensor"),
            P("tensor", None),
            P(),
        ),
        check_vma=False,
    )
```

time: 636 us -> 291 us (0.46)
  waiting for transfers between devices: 455 us -> 141 us
  starting transfers between devices: 0.82 us -> 74.4 us
  blocking collectives: 40.3 us -> 0 us
  matrix products: 65.3 us -> 31.4 us
  other arithmetic: 37.2 us -> 23.7 us
  between operations: 14.8 us -> 3.19 us
  local copies, waits for them, and re-layouts: 21.4 us -> 13.5 us
    psum x2 -> x0, waiting for transfers between devices: 283 us -> none  [the longest x1 188 us: on_device(): grad_w_query, grad_w_out = lax.psum((grad_w_query, grad_w_out), 'dp')]
    ppermute x0 -> x62, waiting for transfers between devices: none -> 141 us  [swap(): return lax.ppermute(values, axis, [(i, i ^ bit) for i in range(size)])]
    reduce_scatter x4 -> x0, waiting for transfers between devices: 99.1 us -> none  [the longest x1 34.6 us: on_device(): lax.psum_scatter(jnp.dot(flat, w_out, preferred_element_type=jnp.float32)...]
    ppermute x0 -> x62, starting transfers between devices: none -> 74.4 us  [swap(): return lax.ppermute(values, axis, [(i, i ^ bit) for i in range(size)])]
    all_gather x4 -> x0, waiting for transfers between devices: 72.3 us -> none  [the longest x1 18.3 us: on_device(): gathered_two = lax.all_gather(normed_two_low, 'tensor', axis=0, tiled=True)]
    psum x1 -> x0, blocking collectives: 40.3 us -> none  [on_device(): lax.psum((grad_w_key, grad_w_value, grad_gain_query, grad_gain_key, grad_...]
    dot_general x35 -> x48, matrix products: 65.3 us -> 31.4 us  [the longest x16 12.5 us: mm_nt(): lax.dot_general(left, right, (((1,), (1,)), ((), ())), preferred_element_...]
    unnamed x105 -> x189, local copies, waits for them, and re-layouts: 13.2 us -> 10.8 us
  transfers between devices with their start and end apart: 10 -> 62, of which waited for: 10 -> 32; matrix products, arithmetic and copies ran while one was open for 3% -> 17% of each run, Pallas kernels for 0% -> 0%
where the time goes in v1:
time: 291 us; the launch traced here: 287 us
  waiting for transfers between devices  141 us (48%)
  starting transfers between devices  74.4 us (26%)
  matrix products  31.4 us (11%)
  other arithmetic  23.7 us (8%)
  local copies, waits for them, and re-layouts  13.5 us (5%)
  between operations  3.19 us (1%)
    ppermute x62, waiting for transfers between devices, swap(): return lax.ppermute(values, axis, [(i, i ^ bit) for i in range(size)])  141 us
    ppermute x62, starting transfers between devices, swap(): return lax.ppermute(values, axis, [(i, i ^ bit) for i in range(size)])  74.4 us
    dot_general x16, matrix products, mm_nt(): lax.dot_general(left, right, (((1,), (1,)), ((), ())), preferred_element_...  12.5 us
    unnamed x189, local copies, waits for them, and re-layouts  10.8 us
    dot_general x16, matrix products, mm(): return jnp.dot(left, right, preferred_element_type=WIDE)  10.1 us
    dot_general x16, matrix products, mm_tn(): lax.dot_general(left, right, (((0,), (0,)), ((), ())), preferred_element_...  8.78 us
  transfers between devices with their start and end apart: 62, of which 32 were waited for; matrix products, arithmetic and copies ran while one was open for 17% of the time, Pallas kernels for 0%

profile of v1, /device:TPU:0, one launch (start us, length us, event | category | flops | bytes accessed | tf_op | source)
XLA Modules:
  0.0 287.5 jit_solution(12673782672675304908)
XLA Ops:
  0.7 3.1 %collective-permute-start.4 = (bf16[640,256]{1,0:T(8,128)(2,1)}, bf16[640,256]{1,0:T(8,128)(2,1)S(1)}, u32[]{:S(2)}, u32[]{:S(2)}) collective-permute-start(bf16[640,256]{1,0:T(8,128)(2,1)} %param.21), channel_id=1, source_target_pairs={{0,2},{1,3},{2,0},{3,1},{4,6},{5,7},{6,4},{7,5},{8,10},{9,11},{10,... | collective-permute-start | bytes 983048 | tf_op jit(solution)/shard_map/ppermute | solution.py:71
  7.9 4.6 %collective-permute-done.4 = bf16[640,256]{1,0:T(8,128)(2,1)S(1)} collective-permute-done((bf16[640,256]{1,0:T(8,128)(2,1)}, bf16[640,256]{1,0:T(8,128)(2,1)S(1)}, u32[]{:S(2)}, u32[]{:S(2)}) %collective-permute-start.4) | collective-permute-done | bytes 327712 | tf_op jit(solution)/shard_map/ppermute | solution.py:71
  15.8 2.1 collective-permute-start.2
  18.0 6.3 %collective-permute-done.2 = bf16[256,512]{0,1:T(8,128)(2,1)S(1)} collective-permute-done((bf16[256,512]{0,1:T(8,128)(2,1)S(1)}, bf16[256,512]{0,1:T(8,128)(2,1)S(1)}, u32[]{:S(2)}, u32[]{:S(2)}) %collective-permute-start.2) | collective-permute-done | bytes 262176 | tf_op jit(solution)/shard_map/ppermute | solution.py:71
  33.5 2.0 collective-permute-done.6
  37.0 1.7 collective-permute-start.8
  39.0 1.7 collective-permute-start.10
  42.1 12.5 %collective-permute-done.8 = bf16[640,512]{1,0:T(8,128)(2,1)S(1)} collective-permute-done((bf16[640,512]{1,0:T(8,128)(2,1)S(1)}, bf16[640,512]{1,0:T(8,128)(2,1)S(1)}, u32[]{:S(2)}, u32[]{:S(2)}) %collective-permute-start.8) | collective-permute-done | bytes 655392 | tf_op jit(solution)/shard_map/ppermute | solution.py:71
  55.8 12.9 %collective-permute-done.9 = bf16[640,512]{1,0:T(8,128)(2,1)S(1)} collective-permute-done((bf16[640,512]{1,0:T(8,128)(2,1)S(1)}, bf16[640,512]{1,0:T(8,128)(2,1)S(1)}, u32[]{:S(2)}, u32[]{:S(2)}) %collective-permute-start.9) | collective-permute-done | bytes 655392 | tf_op jit(solution)/shard_map/ppermute | solution.py:71
  69.4 12.5 %collective-permute-done.10 = bf16[512,640]{1,0:T(8,128)(2,1)S(1)} collective-permute-done((bf16[512,640]{1,0:T(8,128)(2,1)S(1)}, bf16[512,640]{1,0:T(8,128)(2,1)S(1)}, u32[]{:S(2)}, u32[]{:S(2)}) %collective-permute-start.10) | collective-permute-done | bytes 655392 | tf_op jit(solution)/shard_map/ppermute | solution.py:71
  82.6 2.1 collective-permute-done.11
  95.5 1.9 convolution_convert_fusion.2
  97.4 1.8 collective-permute-start.41
  104.7 1.8 collective-permute-start.55
  122.2 6.9 %collective-permute-done.48 = bf16[640,512]{1,0:T(8,128)(2,1)S(1)} collective-permute-done((bf16[640,512]{1,0:T(8,128)(2,1)S(1)}, bf16[640,512]{1,0:T(8,128)(2,1)S(1)}, u32[]{:S(2)}, u32[]{:S(2)}) %collective-permute-start.48) | collective-permute-done | bytes 655392 | tf_op jit(solution)/shard_map/ppermute | solution.py:71
  129.1 1.7 collective-permute-start.34
  131.4 11.8 %collective-permute-done.55 = bf16[512,640]{1,0:T(8,128)(2,1)S(1)} collective-permute-done((bf16[512,640]{1,0:T(8,128)(2,1)S(1)}, bf16[512,640]{1,0:T(8,128)(2,1)S(1)}, u32[]{:S(2)}, u32[]{:S(2)}) %collective-permute-start.55) | collective-permute-done | bytes 655392 | tf_op jit(solution)/shard_map/ppermute | solution.py:71
  145.7 10.9 %collective-permute-done.34 = bf16[256,640]{1,0:T(8,128)(2,1)S(1)} collective-permute-done((bf16[256,640]{1,0:T(8,128)(2,1)S(1)}, bf16[256,640]{1,0:T(8,128)(2,1)S(1)}, u32[]{:S(2)}, u32[]{:S(2)}) %collective-permute-start.34) | collective-permute-done | bytes 327712 | tf_op jit(solution)/shard_map/ppermute | solution.py:71
  156.6 1.7 collective-permute-start.49
  159.2 7.9 %collective-permute-done.49 = bf16[320,512]{1,0:T(8,128)(2,1)S(1)} collective-permute-done((bf16[320,512]{1,0:T(8,128)(2,1)S(1)}, bf16[320,512]{1,0:T(8,128)(2,1)S(1)}, u32[]{:S(2)}, u32[]{:S(2)}) %collective-permute-start.49) | collective-permute-done | bytes 327712 | tf_op jit(solution)/shard_map/ppermute | solution.py:71
  167.2 1.7 collective-permute-start.35
  171.0 3.2 %collective-permute-done.56 = bf16[256,640]{1,0:T(8,128)(2,1)S(1)} collective-permute-done((bf16[256,640]{1,0:T(8,128)(2,1)S(1)}, bf16[256,640]{1,0:T(8,128)(2,1)S(1)}, u32[]{:S(2)}, u32[]{:S(2)}) %collective-permute-start.56) | collective-permute-done | bytes 327712 | tf_op jit(solution)/shard_map/ppermute | solution.py:71
  174.2 1.8 collective-permute-start.50
  176.2 1.8 collective-permute-start.57
  178.5 3.6 %collective-permute-done.50 = bf16[160,512]{1,0:T(8,128)(2,1)S(1)} collective-permute-done((bf16[160,512]{1,0:T(8,128)(2,1)S(1)}, bf16[160,512]{1,0:T(8,128)(2,1)S(1)}, u32[]{:S(2)}, u32[]{:S(2)}) %collective-permute-start.50) | collective-permute-done | bytes 163872 | tf_op jit(solution)/shard_map/ppermute | solution.py:71
  182.1 1.9 collective-permute-start.44
  184.6 3.0 %collective-permute-start.51 = (bf16[80,512]{1,0:T(8,128)(2,1)S(1)}, bf16[80,512]{1,0:T(8,128)(2,1)S(1)}, u32[]{:S(2)}, u32[]{:S(2)}) collective-permute-start(bf16[80,512]{1,0:T(8,128)(2,1)S(1)} %constant_dynamic-slice_fusion.3), channel_id=1, source_target_pairs={{0,16},{4,20},{8,24},{12,28},{16,0},{20,4},{24,8},{28,12},{1,17},{... | collective-permute-start | bytes 245768 | tf_op jit(solution)/shard_map/ppermute | solution.py:71
  189.7 2.6 collective-permute-done.44
  192.6 2.3 collective-permute-done.51
  195.3 2.6 collective-permute-done.37
  198.0 2.9 %collective-permute-start.38 = (bf16[32,640]{1,0:T(8,128)(2,1)S(1)}, bf16[32,640]{1,0:T(8,128)(2,1)S(1)}, u32[]{:S(2)}, u32[]{:S(2)}) collective-permute-start(bf16[32,640]{1,0:T(8,128)(2,1)S(1)} %add_convert_fusion.16), channel_id=1, source_target_pairs={{0,16},{4,20},{8,24},{12,28},{16,0},{20,4},{24,8},{28,12},{1,17},{... | collective-permute-start | bytes 122888 | tf_op jit(solution)/shard_map/ppermute | solution.py:71
  200.9 3.3 %collective-permute-done.38 = bf16[32,640]{1,0:T(8,128)(2,1)S(1)} collective-permute-done((bf16[32,640]{1,0:T(8,128)(2,1)S(1)}, bf16[32,640]{1,0:T(8,128)(2,1)S(1)}, u32[]{:S(2)}, u32[]{:S(2)}) %collective-permute-start.38) | collective-permute-done | bytes 40992 | tf_op jit(solution)/shard_map/ppermute | solution.py:71
  204.2 2.1 collective-permute-start.59
  206.4 3.1 %collective-permute-start.39 = (bf16[64,640]{1,0:T(8,128)(2,1)S(1)}, bf16[64,640]{1,0:T(8,128)(2,1)S(1)}, u32[]{:S(2)}, u32[]{:S(2)}) collective-permute-start(bf16[64,640]{1,0:T(8,128)(2,1)S(1)} %maximum_select_fusion.15), channel_id=1, source_target_pairs={{0,8},{4,12},{8,0},{12,4},{16,24},{20,28},{24,16},{28,20},{1,9},{5... | collective-permute-start | bytes 245768 | tf_op jit(solution)/shard_map/ppermute | solution.py:71
  210.0 4.8 %collective-permute-start.53 = (bf16[160,512]{1,0:T(8,128)(2,1)S(1)}, bf16[160,512]{1,0:T(8,128)(2,1)S(1)}, u32[]{:S(2)}, u32[]{:S(2)}) collective-permute-start(bf16[160,512]{1,0:T(8,128)(2,1)S(1)} %maximum_select_fusion.13), channel_id=1, source_target_pairs={{0,8},{4,12},{8,0},{12,4},{16,24},{20,28},{24,16},{28,20},{1,9},{5... | collective-permute-start | bytes 491528 | tf_op jit(solution)/shard_map/ppermute | solution.py:71
  218.7 3.3 %collective-permute-start.25 = (bf16[640,128]{0,1:T(8,128)(2,1)S(1)}, bf16[640,128]{0,1:T(8,128)(2,1)S(1)}, u32[]{:S(2)}, u32[]{:S(2)}) collective-permute-start(bf16[640,128]{0,1:T(8,128)(2,1)S(1)} %dynamic-slice_convert_fusion), channel_id=1, source_target_pairs={{0,2},{1,3},{2,0},{3,1},{4,6},{5,7},{6,4},{7,5},{8,10},{9,11},{10,... | collective-permute-start | bytes 491528 | tf_op jit(solution)/shard_map/ppermute | solution.py:71
  222.0 4.8 %collective-permute-done.25 = bf16[640,128]{0,1:T(8,128)(2,1)S(1)} collective-permute-done((bf16[640,128]{0,1:T(8,128)(2,1)S(1)}, bf16[640,128]{0,1:T(8,128)(2,1)S(1)}, u32[]{:S(2)}, u32[]{:S(2)}) %collective-permute-start.25) | collective-permute-done | bytes 163872 | tf_op jit(solution)/shard_map/ppermute | solution.py:71
  227.1 1.9 collective-permute-start.26
  230.3 6.8 %collective-permute-done.26 = bf16[320,384]{0,1:T(8,128)(2,1)S(1)} collective-permute-done((bf16[320,384]{0,1:T(8,128)(2,1)S(1)}, bf16[320,384]{0,1:T(8,128)(2,1)S(1)}, u32[]{:S(2)}, u32[]{:S(2)}) %collective-permute-start.26) | collective-permute-done | bytes 245792 | tf_op jit(solution)/shard_map/ppermute | solution.py:71
  237.1 1.7 collective-permute-start.19
  243.5 2.2 collective-permute-done.20
  248.7 1.8 collective-permute-start.28
  250.9 2.1 collective-permute-start.54
  253.1 4.2 %collective-permute-done.28 = bf16[80,384]{0,1:T(8,128)(2,1)S(1)} collective-permute-done((bf16[80,384]{0,1:T(8,128)(2,1)S(1)}, bf16[80,384]{0,1:T(8,128)(2,1)S(1)}, u32[]{:S(2)}, u32[]{:S(2)}) %collective-permute-start.28) | collective-permute-done | bytes 61472 | tf_op jit(solution)/shard_map/ppermute | solution.py:71
  257.4 3.0 %collective-permute-start.29 = (bf16[80,384]{0,1:T(8,128)(2,1)S(1)}, bf16[80,384]{0,1:T(8,128)(2,1)S(1)}, u32[]{:S(2)}, u32[]{:S(2)}) collective-permute-start(bf16[80,384]{0,1:T(8,128)(2,1)S(1)} %add_convert_fusion.10), channel_id=1, source_target_pairs={{0,16},{4,20},{8,24},{12,28},{16,0},{20,4},{24,8},{28,12},{1,17},{... | collective-permute-start | bytes 184328 | tf_op jit(solution)/shard_map/ppermute | solution.py:71
  263.4 2.4 collective-permute-start.30
  266.4 3.0 %collective-permute-done.30 = bf16[160,384]{0,1:T(8,128)(2,1)S(1)} collective-permute-done((bf16[160,384]{0,1:T(8,128)(2,1)S(1)}, bf16[160,384]{0,1:T(8,128)(2,1)S(1)}, u32[]{:S(2)}, u32[]{:S(2)}) %collective-permute-start.30) | collective-permute-done | bytes 122912 | tf_op jit(solution)/shard_map/ppermute | solution.py:71
  272.7 3.8 %collective-permute-done.31 = bf16[320,384]{0,1:T(8,128)(2,1)S(1)} collective-permute-done((bf16[320,384]{0,1:T(8,128)(2,1)S(1)}, bf16[320,384]{0,1:T(8,128)(2,1)S(1)}, u32[]{:S(2)}, u32[]{:S(2)}) %collective-permute-start.31) | collective-permute-done | bytes 245792 | tf_op jit(solution)/shard_map/ppermute | solution.py:71
  (442 shorter events, 94.8 us)
Async XLA Ops:
  0.7 11.8 %collective-permute-start.4 = (bf16[640,256]{1,0:T(8,128)(2,1)}, bf16[640,256]{1,0:T(8,128)(2,1)S(1)}, u32[]{:S(2)}, u32[]{:S(2)}) collective-permute-start(bf16[640,256]{1,0:T(8,128)(2,1)} %param.21), channel_id=1, source_target_pairs={{0,2},{1,3},{2,0},{3,1},{4,6},{5,7},{6,4},{7,5},{8,10},{9,11},{10,... | collective-permute-start | bytes 983048 | tf_op jit(solution)/shard_map/ppermute | solution.py:71
  6.7 5.8 %collective-permute-start = (bf16[256,640]{1,0:T(8,128)(2,1)S(1)}, bf16[256,640]{1,0:T(8,128)(2,1)S(1)}, u32[]{:S(2)}, u32[]{:S(2)}) collective-permute-start(bf16[256,640]{1,0:T(8,128)(2,1)S(1)} %multiply_convert_fusion.9), channel_id=1, source_target_pairs={{0,1},{1,0},{2,3},{3,2},{4,5},{5,4},{6,7},{7,6},{8,9},{9,8},{10,11... | collective-permute-start | bytes 983048 | tf_op jit(solution)/shard_map/ppermute | solution.py:71
  6.8 24.9 %collective-permute-start.5 = (bf16[256,640]{1,0:T(8,128)(2,1)}, bf16[256,640]{1,0:T(8,128)(2,1)}, u32[]{:S(2)}, u32[]{:S(2)}) collective-permute-start(bf16[256,640]{1,0:T(8,128)(2,1)} %param.26), channel_id=1, source_target_pairs={{0,2},{1,3},{2,0},{3,1},{4,6},{5,7},{6,4},{7,5},{8,10},{9,11},{10,... | collective-permute-start | bytes 983048 | tf_op jit(solution)/shard_map/ppermute | solution.py:71
  15.8 8.5 %collective-permute-start.2 = (bf16[256,512]{0,1:T(8,128)(2,1)S(1)}, bf16[256,512]{0,1:T(8,128)(2,1)S(1)}, u32[]{:S(2)}, u32[]{:S(2)}) collective-permute-start(bf16[256,512]{0,1:T(8,128)(2,1)S(1)} %pad_maximum_fusion.10), channel_id=1, source_target_pairs={{0,2},{1,3},{2,0},{3,1},{4,6},{5,7},{6,4},{7,5},{8,10},{9,11},{10,... | collective-permute-start | bytes 786440 | tf_op jit(solution)/shard_map/ppermute | solution.py:71
  17.9 6.4 %collective-permute-start.1 = (bf16[256,512]{0,1:T(8,128)(2,1)S(1)}, bf16[256,512]{0,1:T(8,128)(2,1)S(1)}, u32[]{:S(2)}, u32[]{:S(2)}) collective-permute-start(bf16[256,512]{0,1:T(8,128)(2,1)S(1)} %pad_maximum_fusion.10), channel_id=1, source_target_pairs={{0,1},{1,0},{2,3},{3,2},{4,5},{5,4},{6,7},{7,6},{8,9},{9,8},{10,11... | collective-permute-start | bytes 786440 | tf_op jit(solution)/shard_map/ppermute | solution.py:71
  37.0 17.6 %collective-permute-start.8 = (bf16[640,512]{1,0:T(8,128)(2,1)S(1)}, bf16[640,512]{1,0:T(8,128)(2,1)S(1)}, u32[]{:S(2)}, u32[]{:S(2)}) collective-permute-start(bf16[640,512]{1,0:T(8,128)(2,1)S(1)} %copy-done.30), channel_id=1, source_target_pairs={{0,2},{1,3},{2,0},{3,1},{4,6},{5,7},{6,4},{7,5},{8,10},{9,11},{10,... | collective-permute-start | bytes 1966088 | tf_op jit(solution)/shard_map/ppermute | solution.py:71
  38.7 29.9 %collective-permute-start.9 = (bf16[640,512]{1,0:T(8,128)(2,1)S(1)}, bf16[640,512]{1,0:T(8,128)(2,1)S(1)}, u32[]{:S(2)}, u32[]{:S(2)}) collective-permute-start(bf16[640,512]{1,0:T(8,128)(2,1)S(1)} %copy-done.31), channel_id=1, source_target_pairs={{0,2},{1,3},{2,0},{3,1},{4,6},{5,7},{6,4},{7,5},{8,10},{9,11},{10,... | collective-permute-start | bytes 1966088 | tf_op jit(solution)/shard_map/ppermute | solution.py:71
  39.0 42.8 %collective-permute-start.10 = (bf16[512,640]{1,0:T(8,128)(2,1)S(1)}, bf16[512,640]{1,0:T(8,128)(2,1)S(1)}, u32[]{:S(2)}, u32[]{:S(2)}) collective-permute-start(bf16[512,640]{1,0:T(8,128)(2,1)S(1)} %copy-done.29), channel_id=1, source_target_pairs={{0,2},{1,3},{2,0},{3,1},{4,6},{5,7},{6,4},{7,5},{8,10},{9,11},{10,... | collective-permute-start | bytes 1966088 | tf_op jit(solution)/shard_map/ppermute | solution.py:71
  97.4 23.5 %collective-permute-start.41 = (bf16[640,512]{1,0:T(8,128)(2,1)S(1)}, bf16[640,512]{1,0:T(8,128)(2,1)S(1)}, u32[]{:S(2)}, u32[]{:S(2)}) collective-permute-start(bf16[640,512]{1,0:T(8,128)(2,1)S(1)} %convolution_convert_fusion.2), channel_id=1, source_target_pairs={{0,2},{1,3},{2,0},{3,1},{4,6},{5,7},{6,4},{7,5},{8,10},{9,11},{10,... | collective-permute-start | bytes 1966088 | tf_op jit(solution)/shard_map/ppermute | solution.py:71
  103.7 25.4 %collective-permute-start.48 = (bf16[640,512]{1,0:T(8,128)(2,1)S(1)}, bf16[640,512]{1,0:T(8,128)(2,1)S(1)}, u32[]{:S(2)}, u32[]{:S(2)}) collective-permute-start(bf16[640,512]{1,0:T(8,128)(2,1)S(1)} %convolution_convert_fusion.1), channel_id=1, source_target_pairs={{0,2},{1,3},{2,0},{3,1},{4,6},{5,7},{6,4},{7,5},{8,10},{9,11},{10,... | collective-permute-start | bytes 1966088 | tf_op jit(solution)/shard_map/ppermute | solution.py:71
  104.7 38.5 %collective-permute-start.55 = (bf16[512,640]{1,0:T(8,128)(2,1)S(1)}, bf16[512,640]{1,0:T(8,128)(2,1)S(1)}, u32[]{:S(2)}, u32[]{:S(2)}) collective-permute-start(bf16[512,640]{1,0:T(8,128)(2,1)S(1)} %convolution_convert_fusion), channel_id=1, source_target_pairs={{0,2},{1,3},{2,0},{3,1},{4,6},{5,7},{6,4},{7,5},{8,10},{9,11},{10,... | collective-permute-start | bytes 1966088 | tf_op jit(solution)/shard_map/ppermute | solution.py:71
  115.9 71.8 %collective-permute-start.16 = (bf16[512,512]{0,1:T(8,128)(2,1)S(1)}, bf16[512,512]{0,1:T(8,128)(2,1)S(1)}, u32[]{:S(2)}, u32[]{:S(2)}) collective-permute-start(bf16[512,512]{0,1:T(8,128)(2,1)S(1)} %pad_maximum_fusion.8), channel_id=1, source_target_pairs={{0,1},{1,0},{2,3},{3,2},{4,5},{5,4},{6,7},{7,6},{8,9},{9,8},{10,11... | collective-permute-start | bytes 1572872 | tf_op jit(solution)/shard_map/ppermute | solution.py:71
  120.0 97.7 %collective-permute-start.15 = (bf16[256,640]{1,0:T(8,128)(2,1)S(1)}, bf16[256,640]{1,0:T(8,128)(2,1)S(1)}, u32[]{:S(2)}, u32[]{:S(2)}) collective-permute-start(bf16[256,640]{1,0:T(8,128)(2,1)S(1)} %slice.324), channel_id=1, source_target_pairs={{0,1},{1,0},{2,3},{3,2},{4,5},{5,4},{6,7},{7,6},{8,9},{9,8},{10,11... | collective-permute-start | bytes 983048 | tf_op jit(solution)/shard_map/ppermute | solution.py:71
  120.9 48.2 %collective-permute-start.23 = (bf16[640,256]{0,1:T(8,128)(2,1)S(1)}, bf16[640,256]{0,1:T(8,128)(2,1)S(1)}, u32[]{:S(2)}, u32[]{:S(2)}) collective-permute-start(bf16[640,256]{0,1:T(8,128)(2,1)S(1)} %convolution_convert_fusion.3), channel_id=1, source_target_pairs={{0,2},{1,3},{2,0},{3,1},{4,6},{5,7},{6,4},{7,5},{8,10},{9,11},{10,... | collective-permute-start | bytes 983048 | tf_op jit(solution)/shard_map/ppermute | solution.py:71
  129.1 27.5 %collective-permute-start.34 = (bf16[256,640]{1,0:T(8,128)(2,1)S(1)}, bf16[256,640]{1,0:T(8,128)(2,1)S(1)}, u32[]{:S(2)}, u32[]{:S(2)}) collective-permute-start(bf16[256,640]{1,0:T(8,128)(2,1)S(1)} %convolution_convert_fusion.4), channel_id=1, source_target_pairs={{0,2},{1,3},{2,0},{3,1},{4,6},{5,7},{6,4},{7,5},{8,10},{9,11},{10,... | collective-permute-start | bytes 983048 | tf_op jit(solution)/shard_map/ppermute | solution.py:71
  143.1 15.6 %collective-permute-start.42 = (bf16[320,512]{1,0:T(8,128)(2,1)S(1)}, bf16[320,512]{1,0:T(8,128)(2,1)S(1)}, u32[]{:S(2)}, u32[]{:S(2)}) collective-permute-start(bf16[320,512]{1,0:T(8,128)(2,1)S(1)} %constant_dynamic-slice_fusion.8), channel_id=1, source_target_pairs={{0,4},{4,0},{8,12},{12,8},{16,20},{20,16},{24,28},{28,24},{1,5},{5... | collective-permute-start | bytes 983048 | tf_op jit(solution)/shard_map/ppermute | solution.py:71
  156.6 10.6 %collective-permute-start.49 = (bf16[320,512]{1,0:T(8,128)(2,1)S(1)}, bf16[320,512]{1,0:T(8,128)(2,1)S(1)}, u32[]{:S(2)}, u32[]{:S(2)}) collective-permute-start(bf16[320,512]{1,0:T(8,128)(2,1)S(1)} %constant_dynamic-slice_fusion.5), channel_id=1, source_target_pairs={{0,4},{4,0},{8,12},{12,8},{16,20},{20,16},{24,28},{28,24},{1,5},{5... | collective-permute-start | bytes 983048 | tf_op jit(solution)/shard_map/ppermute | solution.py:71
  158.7 15.4 %collective-permute-start.56 = (bf16[256,640]{1,0:T(8,128)(2,1)S(1)}, bf16[256,640]{1,0:T(8,128)(2,1)S(1)}, u32[]{:S(2)}, u32[]{:S(2)}) collective-permute-start(bf16[256,640]{1,0:T(8,128)(2,1)S(1)} %constant_dynamic-slice_fusion.2), channel_id=1, source_target_pairs={{0,4},{4,0},{8,12},{12,8},{16,20},{20,16},{24,28},{28,24},{1,5},{5... | collective-permute-start | bytes 983048 | tf_op jit(solution)/shard_map/ppermute | solution.py:71
  167.2 9.1 %collective-permute-start.35 = (bf16[128,640]{1,0:T(8,128)(2,1)S(1)}, bf16[128,640]{1,0:T(8,128)(2,1)S(1)}, u32[]{:S(2)}, u32[]{:S(2)}) collective-permute-start(bf16[128,640]{1,0:T(8,128)(2,1)S(1)} %constant_dynamic-slice_fusion.11), channel_id=1, source_target_pairs={{0,4},{4,0},{8,12},{12,8},{16,20},{20,16},{24,28},{28,24},{1,5},{5... | collective-permute-start | bytes 491528 | tf_op jit(solution)/shard_map/ppermute | solution.py:71
  169.0 9.1 %collective-permute-start.43 = (bf16[160,512]{1,0:T(8,128)(2,1)S(1)}, bf16[160,512]{1,0:T(8,128)(2,1)S(1)}, u32[]{:S(2)}, u32[]{:S(2)}) collective-permute-start(bf16[160,512]{1,0:T(8,128)(2,1)S(1)} %constant_dynamic-slice_fusion.7), channel_id=1, source_target_pairs={{0,8},{4,12},{8,0},{12,4},{16,24},{20,28},{24,16},{28,20},{1,9},{5... | collective-permute-start | bytes 491528 | tf_op jit(solution)/shard_map/ppermute | solution.py:71
  174.2 8.0 %collective-permute-start.50 = (bf16[160,512]{1,0:T(8,128)(2,1)S(1)}, bf16[160,512]{1,0:T(8,128)(2,1)S(1)}, u32[]{:S(2)}, u32[]{:S(2)}) collective-permute-start(bf16[160,512]{1,0:T(8,128)(2,1)S(1)} %constant_dynamic-slice_fusion.4), channel_id=1, source_target_pairs={{0,8},{4,12},{8,0},{12,4},{16,24},{20,28},{24,16},{28,20},{1,9},{5... | collective-permute-start | bytes 491528 | tf_op jit(solution)/shard_map/ppermute | solution.py:71
  176.2 8.3 %collective-permute-start.57 = (bf16[128,640]{1,0:T(8,128)(2,1)S(1)}, bf16[128,640]{1,0:T(8,128)(2,1)S(1)}, u32[]{:S(2)}, u32[]{:S(2)}) collective-permute-start(bf16[128,640]{1,0:T(8,128)(2,1)S(1)} %constant_dynamic-slice_fusion.1), channel_id=1, source_target_pairs={{0,8},{4,12},{8,0},{12,4},{16,24},{20,28},{24,16},{28,20},{1,9},{5... | collective-permute-start | bytes 491528 | tf_op jit(solution)/shard_map/ppermute | solution.py:71
  178.1 9.8 %collective-permute-start.36 = (bf16[64,640]{1,0:T(8,128)(2,1)S(1)}, bf16[64,640]{1,0:T(8,128)(2,1)S(1)}, u32[]{:S(2)}, u32[]{:S(2)}) collective-permute-start(bf16[64,640]{1,0:T(8,128)(2,1)S(1)} %constant_dynamic-slice_fusion.10), channel_id=1, source_target_pairs={{0,8},{4,12},{8,0},{12,4},{16,24},{20,28},{24,16},{28,20},{1,9},{5... | collective-permute-start | bytes 245768 | tf_op jit(solution)/shard_map/ppermute | solution.py:71
  182.1 10.1 %collective-permute-start.44 = (bf16[80,512]{1,0:T(8,128)(2,1)S(1)}, bf16[80,512]{1,0:T(8,128)(2,1)S(1)}, u32[]{:S(2)}, u32[]{:S(2)}) collective-permute-start(bf16[80,512]{1,0:T(8,128)(2,1)S(1)} %constant_dynamic-slice_fusion.6), channel_id=1, source_target_pairs={{0,16},{4,20},{8,24},{12,28},{16,0},{20,4},{24,8},{28,12},{1,17},{... | collective-permute-start | bytes 245768 | tf_op jit(solution)/shard_map/ppermute | solution.py:71
  184.6 10.4 %collective-permute-start.51 = (bf16[80,512]{1,0:T(8,128)(2,1)S(1)}, bf16[80,512]{1,0:T(8,128)(2,1)S(1)}, u32[]{:S(2)}, u32[]{:S(2)}) collective-permute-start(bf16[80,512]{1,0:T(8,128)(2,1)S(1)} %constant_dynamic-slice_fusion.3), channel_id=1, source_target_pairs={{0,16},{4,20},{8,24},{12,28},{16,0},{20,4},{24,8},{28,12},{1,17},{... | collective-permute-start | bytes 245768 | tf_op jit(solution)/shard_map/ppermute | solution.py:71
  187.7 10.3 %collective-permute-start.58 = (bf16[64,640]{1,0:T(8,128)(2,1)S(1)}, bf16[64,640]{1,0:T(8,128)(2,1)S(1)}, u32[]{:S(2)}, u32[]{:S(2)}) collective-permute-start(bf16[64,640]{1,0:T(8,128)(2,1)S(1)} %constant_dynamic-slice_fusion), channel_id=1, source_target_pairs={{0,16},{4,20},{8,24},{12,28},{16,0},{20,4},{24,8},{28,12},{1,17},{... | collective-permute-start | bytes 245768 | tf_op jit(solution)/shard_map/ppermute | solution.py:71
  188.0 27.0 %collective-permute-start.17 = (bf16[256,512]{0,1:T(8,128)(2,1)S(1)}, bf16[256,512]{0,1:T(8,128)(2,1)S(1)}, u32[]{:S(2)}, u32[]{:S(2)}) collective-permute-start(bf16[256,512]{0,1:T(8,128)(2,1)S(1)} %slice.326), channel_id=1, source_target_pairs={{0,2},{1,3},{2,0},{3,1},{4,6},{5,7},{6,4},{7,5},{8,10},{9,11},{10,... | collective-permute-start | bytes 786440 | tf_op jit(solution)/shard_map/ppermute | solution.py:71
  192.3 5.6 %collective-permute-start.37 = (bf16[32,640]{1,0:T(8,128)(2,1)S(1)}, bf16[32,640]{1,0:T(8,128)(2,1)S(1)}, u32[]{:S(2)}, u32[]{:S(2)}) collective-permute-start(bf16[32,640]{1,0:T(8,128)(2,1)S(1)} %constant_dynamic-slice_fusion.9), channel_id=1, source_target_pairs={{0,16},{4,20},{8,24},{12,28},{16,0},{20,4},{24,8},{28,12},{1,17},{... | collective-permute-start | bytes 122888 | tf_op jit(solution)/shard_map/ppermute | solution.py:71
  194.9 11.5 %collective-permute-start.45 = (bf16[80,512]{1,0:T(8,128)(2,1)S(1)}, bf16[80,512]{1,0:T(8,128)(2,1)S(1)}, u32[]{:S(2)}, u32[]{:S(2)}) collective-permute-start(bf16[80,512]{1,0:T(8,128)(2,1)S(1)} %add_convert_fusion.13), channel_id=1, source_target_pairs={{0,16},{4,20},{8,24},{12,28},{16,0},{20,4},{24,8},{28,12},{1,17},{... | collective-permute-start | bytes 245768 | tf_op jit(solution)/shard_map/ppermute | solution.py:71
  197.9 11.6 %collective-permute-start.52 = (bf16[80,512]{1,0:T(8,128)(2,1)S(1)}, bf16[80,512]{1,0:T(8,128)(2,1)S(1)}, u32[]{:S(2)}, u32[]{:S(2)}) collective-permute-start(bf16[80,512]{1,0:T(8,128)(2,1)S(1)} %add_convert_fusion.12), channel_id=1, source_target_pairs={{0,16},{4,20},{8,24},{12,28},{16,0},{20,4},{24,8},{28,12},{1,17},{... | collective-permute-start | bytes 245768 | tf_op jit(solution)/shard_map/ppermute | solution.py:71
  198.0 6.2 %collective-permute-start.38 = (bf16[32,640]{1,0:T(8,128)(2,1)S(1)}, bf16[32,640]{1,0:T(8,128)(2,1)S(1)}, u32[]{:S(2)}, u32[]{:S(2)}) collective-permute-start(bf16[32,640]{1,0:T(8,128)(2,1)S(1)} %add_convert_fusion.16), channel_id=1, source_target_pairs={{0,16},{4,20},{8,24},{12,28},{16,0},{20,4},{24,8},{28,12},{1,17},{... | collective-permute-start | bytes 122888 | tf_op jit(solution)/shard_map/ppermute | solution.py:71
  204.2 5.8 %collective-permute-start.59 = (bf16[64,640]{1,0:T(8,128)(2,1)S(1)}, bf16[64,640]{1,0:T(8,128)(2,1)S(1)}, u32[]{:S(2)}, u32[]{:S(2)}) collective-permute-start(bf16[64,640]{1,0:T(8,128)(2,1)S(1)} %add_convert_fusion.11), channel_id=1, source_target_pairs={{0,16},{4,20},{8,24},{12,28},{16,0},{20,4},{24,8},{28,12},{1,17},{... | collective-permute-start | bytes 245768 | tf_op jit(solution)/shard_map/ppermute | solution.py:71
  206.4 8.4 %collective-permute-start.39 = (bf16[64,640]{1,0:T(8,128)(2,1)S(1)}, bf16[64,640]{1,0:T(8,128)(2,1)S(1)}, u32[]{:S(2)}, u32[]{:S(2)}) collective-permute-start(bf16[64,640]{1,0:T(8,128)(2,1)S(1)} %maximum_select_fusion.15), channel_id=1, source_target_pairs={{0,8},{4,12},{8,0},{12,4},{16,24},{20,28},{24,16},{28,20},{1,9},{5... | collective-permute-start | bytes 245768 | tf_op jit(solution)/shard_map/ppermute | solution.py:71
  209.5 32.3 %collective-permute-start.46 = (bf16[160,512]{1,0:T(8,128)(2,1)S(1)}, bf16[160,512]{1,0:T(8,128)(2,1)S(1)}, u32[]{:S(2)}, u32[]{:S(2)}) collective-permute-start(bf16[160,512]{1,0:T(8,128)(2,1)S(1)} %maximum_select_fusion.12), channel_id=1, source_target_pairs={{0,8},{4,12},{8,0},{12,4},{16,24},{20,28},{24,16},{28,20},{1,9},{5... | collective-permute-start | bytes 491528 | tf_op jit(solution)/shard_map/ppermute | solution.py:71
  210.0 38.7 %collective-permute-start.53 = (bf16[160,512]{1,0:T(8,128)(2,1)S(1)}, bf16[160,512]{1,0:T(8,128)(2,1)S(1)}, u32[]{:S(2)}, u32[]{:S(2)}) collective-permute-start(bf16[160,512]{1,0:T(8,128)(2,1)S(1)} %maximum_select_fusion.13), channel_id=1, source_target_pairs={{0,8},{4,12},{8,0},{12,4},{16,24},{20,28},{24,16},{28,20},{1,9},{5... | collective-permute-start | bytes 491528 | tf_op jit(solution)/shard_map/ppermute | solution.py:71
  214.8 42.5 %collective-permute-start.60 = (bf16[128,640]{1,0:T(8,128)(2,1)S(1)}, bf16[128,640]{1,0:T(8,128)(2,1)S(1)}, u32[]{:S(2)}, u32[]{:S(2)}) collective-permute-start(bf16[128,640]{1,0:T(8,128)(2,1)S(1)} %maximum_select_fusion.14), channel_id=1, source_target_pairs={{0,8},{4,12},{8,0},{12,4},{16,24},{20,28},{24,16},{28,20},{1,9},{5... | collective-permute-start | bytes 491528 | tf_op jit(solution)/shard_map/ppermute | solution.py:71
  218.4 11.6 %collective-permute-start.18 = (f32[24,128]{1,0:T(8,128)S(1)}, f32[24,128]{1,0:T(8,128)S(1)}, u32[]{:S(2)}, u32[]{:S(2)}) collective-permute-start(f32[24,128]{1,0:T(8,128)S(1)} %bitcast.120), channel_id=1, source_target_pairs={{0,1},{1,0},{2,3},{3,2},{4,5},{5,4},{6,7},{7,6},{8,9},{9,8},{10,11... | collective-permute-start | bytes 36872 | tf_op jit(solution)/shard_map/ppermute | solution.py:71
  218.7 8.1 %collective-permute-start.25 = (bf16[640,128]{0,1:T(8,128)(2,1)S(1)}, bf16[640,128]{0,1:T(8,128)(2,1)S(1)}, u32[]{:S(2)}, u32[]{:S(2)}) collective-permute-start(bf16[640,128]{0,1:T(8,128)(2,1)S(1)} %dynamic-slice_convert_fusion), channel_id=1, source_target_pairs={{0,2},{1,3},{2,0},{3,1},{4,6},{5,7},{6,4},{7,5},{8,10},{9,11},{10,... | collective-permute-start | bytes 491528 | tf_op jit(solution)/shard_map/ppermute | solution.py:71
  227.1 9.9 %collective-permute-start.26 = (bf16[320,384]{0,1:T(8,128)(2,1)S(1)}, bf16[320,384]{0,1:T(8,128)(2,1)S(1)}, u32[]{:S(2)}, u32[]{:S(2)}) collective-permute-start(bf16[320,384]{0,1:T(8,128)(2,1)S(1)} %fusion.70), channel_id=1, source_target_pairs={{0,4},{4,0},{8,12},{12,8},{16,20},{20,16},{24,28},{28,24},{1,5},{5... | collective-permute-start | bytes 737288 | tf_op jit(solution)/shard_map/ppermute | solution.py:71
  230.0 41.8 %collective-permute-start.40 = (bf16[128,640]{1,0:T(8,128)(2,1)S(1)}, bf16[128,640]{1,0:T(8,128)(2,1)S(1)}, u32[]{:S(2)}, u32[]{:S(2)}) collective-permute-start(bf16[128,640]{1,0:T(8,128)(2,1)S(1)} %maximum_select_fusion.11), channel_id=1, source_target_pairs={{0,4},{4,0},{8,12},{12,8},{16,20},{20,16},{24,28},{28,24},{1,5},{5... | collective-permute-start | bytes 491528 | tf_op jit(solution)/shard_map/ppermute | solution.py:71
  240.8 6.5 %collective-permute-start.27 = (bf16[160,384]{0,1:T(8,128)(2,1)S(1)}, bf16[160,384]{0,1:T(8,128)(2,1)S(1)}, u32[]{:S(2)}, u32[]{:S(2)}) collective-permute-start(bf16[160,384]{0,1:T(8,128)(2,1)S(1)} %constant_dynamic-slice_fusion.13), channel_id=1, source_target_pairs={{0,8},{4,12},{8,0},{12,4},{16,24},{20,28},{24,16},{28,20},{1,9},{5... | collective-permute-start | bytes 368648 | tf_op jit(solution)/shard_map/ppermute | solution.py:71
  245.7 32.9 %collective-permute-start.47 = (bf16[320,512]{1,0:T(8,128)(2,1)S(1)}, bf16[320,512]{1,0:T(8,128)(2,1)S(1)}, u32[]{:S(2)}, u32[]{:S(2)}) collective-permute-start(bf16[320,512]{1,0:T(8,128)(2,1)S(1)} %maximum_select_fusion.6), channel_id=1, source_target_pairs={{0,4},{4,0},{8,12},{12,8},{16,20},{20,16},{24,28},{28,24},{1,5},{5... | collective-permute-start | bytes 983048 | tf_op jit(solution)/shard_map/ppermute | solution.py:71
  248.7 8.5 %collective-permute-start.28 = (bf16[80,384]{0,1:T(8,128)(2,1)S(1)}, bf16[80,384]{0,1:T(8,128)(2,1)S(1)}, u32[]{:S(2)}, u32[]{:S(2)}) collective-permute-start(bf16[80,384]{0,1:T(8,128)(2,1)S(1)} %constant_dynamic-slice_fusion.12), channel_id=1, source_target_pairs={{0,16},{4,20},{8,24},{12,28},{16,0},{20,4},{24,8},{28,12},{1,17},{... | collective-permute-start | bytes 184328 | tf_op jit(solution)/shard_map/ppermute | solution.py:71
  250.9 28.9 %collective-permute-start.54 = (bf16[320,512]{1,0:T(8,128)(2,1)S(1)}, bf16[320,512]{1,0:T(8,128)(2,1)S(1)}, u32[]{:S(2)}, u32[]{:S(2)}) collective-permute-start(bf16[320,512]{1,0:T(8,128)(2,1)S(1)} %maximum_select_fusion.7), channel_id=1, source_target_pairs={{0,4},{4,0},{8,12},{12,8},{16,20},{20,16},{24,28},{28,24},{1,5},{5... | collective-permute-start | bytes 983048 | tf_op jit(solution)/shard_map/ppermute | solution.py:71
  257.4 5.9 %collective-permute-start.29 = (bf16[80,384]{0,1:T(8,128)(2,1)S(1)}, bf16[80,384]{0,1:T(8,128)(2,1)S(1)}, u32[]{:S(2)}, u32[]{:S(2)}) collective-permute-start(bf16[80,384]{0,1:T(8,128)(2,1)S(1)} %add_convert_fusion.10), channel_id=1, source_target_pairs={{0,16},{4,20},{8,24},{12,28},{16,0},{20,4},{24,8},{28,12},{1,17},{... | collective-permute-start | bytes 184328 | tf_op jit(solution)/shard_map/ppermute | solution.py:71
  261.9 20.4 %collective-permute-start.61 = (bf16[256,640]{1,0:T(8,128)(2,1)S(1)}, bf16[256,640]{1,0:T(8,128)(2,1)S(1)}, u32[]{:S(2)}, u32[]{:S(2)}) collective-permute-start(bf16[256,640]{1,0:T(8,128)(2,1)S(1)} %maximum_select_fusion.8), channel_id=1, source_target_pairs={{0,4},{4,0},{8,12},{12,8},{16,20},{20,16},{24,28},{28,24},{1,5},{5... | collective-permute-start | bytes 983048 | tf_op jit(solution)/shard_map/ppermute | solution.py:71
  263.4 6.0 %collective-permute-start.30 = (bf16[160,384]{0,1:T(8,128)(2,1)S(1)}, bf16[160,384]{0,1:T(8,128)(2,1)S(1)}, u32[]{:S(2)}, u32[]{:S(2)}) collective-permute-start(bf16[160,384]{0,1:T(8,128)(2,1)S(1)} %maximum_select_fusion.10), channel_id=1, source_target_pairs={{0,8},{4,12},{8,0},{12,4},{16,24},{20,28},{24,16},{28,20},{1,9},{5... | collective-permute-start | bytes 368648 | tf_op jit(solution)/shard_map/ppermute | solution.py:71
  269.7 6.8 %collective-permute-start.31 = (bf16[320,384]{0,1:T(8,128)(2,1)S(1)}, bf16[320,384]{0,1:T(8,128)(2,1)S(1)}, u32[]{:S(2)}, u32[]{:S(2)}) collective-permute-start(bf16[320,384]{0,1:T(8,128)(2,1)S(1)} %maximum_select_fusion.9), channel_id=1, source_target_pairs={{0,4},{4,0},{8,12},{12,8},{16,20},{20,16},{24,28},{28,24},{1,5},{5... | collective-permute-start | bytes 737288 | tf_op jit(solution)/shard_map/ppermute | solution.py:71
  (105 other events, 423.0 us)
